TPU v7x, 32 devices: a whole 2x2x4 slice. The times are simulated.
32 devices in a mesh: xy: 8 (over y, x, core), gz: 4 (over z).
Axes of the slice: x: 2, y: 2, z: 4, core: 2. Of those that a mesh axis runs over, the one named last changes fastest.
Arguments:
- velocity: float32 [3, 16, 256, 1024], P(None, 'gz', 'xy'), may hold values from -6 to 6
- magnetic: float32 [3, 8, 128, 512], P(None, 'gz', 'xy'), may hold values from -6 to 6
- slot_block_table: int32 [256], P('xy'), may hold values from 0 to 255, as said below
Outputs:
- updated_fine_velocity: float32 [3, 16, 256, 1024], P(None, 'gz', 'xy')
- magnetic_next: float32 [3, 8, 128, 512], P(None, 'gz', 'xy')
Inputs may be any that keep to these rules, and one draw needn't show every extreme that they name: `slot_block_table`: each block number appears in one slot; the 32 slots of one device along xy hold exactly 4 blocks of every block row.
All inputs are finite; a program needn't handle non-finite values.
Results may differ from a plain program's by a relative error of at most 0.00005.
Values sent between devices are 32-bit elements; how exact they have to be, the bound alone decides.
No kernel may reach another device: no remote copies, remote signals or barrier semaphores. Data moves between devices by JAX's collectives and lax.ppermute only.
A program may use at most 64 MiB of HBM per device.

v0:
```python
import jax
import jax.numpy as jnp
from jax import lax
from jax.sharding import PartitionSpec as P

BLOCK_EDGE = 32


def with_halo(value, sides, width):
    for axis, dim in sides:
        size, length = (lax.axis_size(axis), value.shape[dim])
        up = [(i, (i + 1) % size) for i in range(size)]
        down = [(j, i) for i, j in up]
        last = lax.slice_in_dim(value, length - width, length, axis=dim)
        first = lax.slice_in_dim(value, 0, width, axis=dim)
        before = lax.ppermute(last, axis, up)
        after = lax.ppermute(first, axis, down)
        value = jnp.concatenate([before, value, after], axis=dim)
    return value


def restrict(fine, blk):
    half_width = blk // 2
    s = fine.shape
    v = fine.reshape(s[0], s[1] // 2, 2, s[2], half_width, 2, half_width, 2)
    return (jnp.sum(v, axis=(2, 5, 7)) * 0.125).reshape(
        s[0], s[1] // 2, s[2], half_width * half_width
    )


def inner(padded):
    return padded[:, 1:-1, 1:-1]


def along_z(padded):
    return (padded[:, 2:, 1:-1] - padded[:, :-2, 1:-1]) * 0.5


def along_y(padded):
    return (padded[:, 1:-1, 2:] - padded[:, 1:-1, :-2]) * 0.5


def along_x(padded):
    middle = inner(padded)
    return (jnp.roll(middle, -1, 3) - jnp.roll(middle, 1, 3)) * 0.5


def curl_padded(padded):
    dzv = along_z(padded)
    dyv = along_y(padded)
    dxv = along_x(padded)
    return jnp.stack([dyv[2] - dzv[1], dzv[0] - dxv[2], dxv[1] - dyv[0]])


def cross(a, b):
    return jnp.stack(
        [a[1] * b[2] - a[2] * b[1], a[2] * b[0] - a[0] * b[2], a[0] * b[1] - a[1] * b[0]]
    )


def laplace_padded(padded):
    middle = inner(padded)
    total = padded[:, 2:, 1:-1] + padded[:, :-2, 1:-1] + padded[:, 1:-1, 2:] + padded[:, 1:-1, :-2]
    return total + jnp.roll(middle, 1, 3) + jnp.roll(middle, -1, 3) - 6.0 * middle


def split_into_tiles(magnetic_state, coarse_depth_index, half_width, slot_count):
    return (
        magnetic_state.reshape(
            magnetic_state.shape[0], coarse_depth_index, half_width, slot_count, half_width
        )
        .transpose(0, 1, 3, 2, 4)
        .reshape(magnetic_state.shape[0], coarse_depth_index, slot_count, half_width * half_width)
    )


def assemble_from_tiles(tile_stack, coarse_depth_index, half_width, slot_count):
    return (
        tile_stack.reshape(
            tile_stack.shape[0], coarse_depth_index, slot_count, half_width, half_width
        )
        .transpose(0, 1, 3, 2, 4)
        .reshape(tile_stack.shape[0], coarse_depth_index, half_width, slot_count * half_width)
    )


def body(velocity, magnetic, slot_block_table):
    half_width = BLOCK_EDGE // 2
    slot_count = velocity.shape[2]
    coarse_depth_index = velocity.shape[1] // 2
    column_indices = slot_block_table % slot_count
    sorted_positions = jnp.argsort(slot_block_table)
    dispatched_columns = column_indices[sorted_positions].reshape(1, 1, slot_count, 1)
    ordered = velocity[:, :, sorted_positions]
    got, received_columns = (
        lax.all_to_all(
            restrict(ordered, BLOCK_EDGE), "xy", split_axis=2, concat_axis=2, tiled=True
        ),
        lax.all_to_all(dispatched_columns, "xy", split_axis=2, concat_axis=2, tiled=True),
    )
    column_listing = received_columns.reshape(slot_count)
    grouped_by_column = got[:, :, jnp.argsort(column_listing)]
    coarse_flow_field = assemble_from_tiles(
        grouped_by_column, coarse_depth_index, half_width, slot_count
    )
    emf = cross(coarse_flow_field, magnetic)
    stacked = jnp.concatenate([magnetic, emf], axis=0)
    padded = with_halo(stacked, (("xy", 2), ("gz", 1)), 1)
    field_pad = padded[0:3]
    current = curl_padded(field_pad)
    magnetic_next = magnetic + 0.1 * (curl_padded(padded[3:6]) + 0.5 * laplace_padded(field_pad))
    lorentz_force = cross(current, magnetic)
    returned_back_tiles = split_into_tiles(
        lorentz_force, coarse_depth_index, half_width, slot_count
    )[:, :, column_listing]
    returned = lax.all_to_all(returned_back_tiles, "xy", split_axis=2, concat_axis=2, tiled=True)
    blocks_per_slot = returned[:, :, jnp.argsort(sorted_positions)]
    widened_tiles = jnp.broadcast_to(
        blocks_per_slot.reshape(3, coarse_depth_index, 1, slot_count, half_width, 1, half_width, 1),
        (3, coarse_depth_index, 2, slot_count, half_width, 2, half_width, 2),
    )
    updated_fine_velocity = velocity + 0.1 * widened_tiles.reshape(
        3, coarse_depth_index * 2, slot_count, BLOCK_EDGE * BLOCK_EDGE
    )
    return (updated_fine_velocity, magnetic_next)


def solution(mesh):
    return jax.shard_map(
        body,
        mesh=mesh,
        in_specs=(P(None, "gz", "xy", None), P(None, "gz", "xy", None), P("xy")),
        out_specs=(P(None, "gz", "xy", None), P(None, "gz", "xy", None)),
        check_vma=False,
    )
```

profile of v0, /device:TPU:0, one launch (start us, length us, event | category | flops | bytes accessed | tf_op | source)
XLA Modules:
  0.0 104.9 jit_solution(8437130082161293835)
XLA Ops:
  1.4 2.3 %sort.45 = (s32[32]{0:T(128)}, s32[32]{0:T(128)S(1)}) sort(s32[32]{0:T(128)} %param.5, s32[32]{0:T(128)S(1)} %iota.10), dimensions={0}, to_apply=%region_0.1 | sort | flops 160 | bytes 512 | tf_op jit(solution)/shard_map/jit(argsort)/sort | solution.py:92
  5.7 5.2 %all-to-all-start.1 = ((s32[1,1,32,1]{3,1,0,2:T(1,128)}), s32[1,1,32,1]{3,1,0,2:T(1,128)S(1)}, u32[]{:S(2)}, u32[]{:S(2)}) async-start(s32[1,1,32,1]{3,1,0,2:T(1,128)} %copy.33), calls=%async_computation.1 | async-start | bytes 32768 | tf_op jit(solution)/shard_map/all_to_all | solution.py:99
  10.9 1.5 %fusion.14 = (f32[3,2,16,1]{3,2,1,0:T(8,128)}, f32[3,2,16,1]{3,2,1,0:T(8,128)}) fusion(f32[3,2,16,512]{3,2,1,0:T(8,128)} %param.4), kind=kLoop, calls=%fused_computation.82 | loop fusion | bytes 1536 | tf_op jit(solution)/shard_map/jit(_roll_static)/slice | solution.py:45
  13.6 3.0 %gather_fusion = f32[32,3,4,1024]{3,0,2,1:T(8,128)S(1)} fusion(f32[3,4,32,1024]{3,2,1,0:T(8,128)S(1)} %copy-done, s32[1024]{0:T(1024)} %copy-done.18), kind=kCustom, calls=%fused_computation | custom fusion | bytes 3145856 | tf_op jit(solution)/shard_map/gather | solution.py:94
  16.5 4.0 %copy.43 = f32[3,4,32,1024]{2,3,1,0:T(8,128)} copy(f32[3,4,32,1024]{3,2,1,0:T(8,128)S(1)} %copy-done) | data formatting | bytes 3145728 | tf_op args[0]
  20.5 2.3 %sort.47 = (s32[32]{0:T(128)}, s32[32]{0:T(128)S(1)}) sort(s32[32]{0:T(128)} %copy-done.19, s32[32]{0:T(128)S(1)} %iota.12), dimensions={0}, to_apply=%region_3.4 | sort | flops 160 | bytes 512 | tf_op jit(solution)/shard_map/jit(argsort)/sort | solution.py:117
  23.4 4.0 %copy.31 = f32[3,4,32,1024]{2,3,1,0:T(8,128)} copy(f32[3,4,32,1024]{3,2,1,0:T(8,128)S(1)} %bitcast.34) | data formatting | bytes 3145728 | tf_op jit(solution)/shard_map/gather | solution.py:94
  27.3 7.3 %reduce_sum.9 = f32[3,2,32,16,16]{2,4,3,1,0:T(8,128)S(1)} reduce(f32[3,2,2,32,16,2,16,2]{3,7,6,5,4,2,1,0:T(2,128)} %bitcast.32, f32[]{:T(128)} %constant.10.clone.1), dimensions={2,5,7}, to_apply=%region_1.2 | reduce | flops 344064 | bytes 1769476 | tf_op jit(solution)/shard_map/reduce_sum | solution.py:26
  36.5 4.2 %all-to-all-start = ((f32[3,2,32,256]{3,1,0,2:T(2,128)}), f32[3,2,32,256]{3,1,0,2:T(2,128)S(1)}, u32[]{:S(2)}, u32[]{:S(2)}) async-start(f32[3,2,32,256]{3,1,0,2:T(2,128)} %copy.32), calls=%async_computation | async-start | bytes 393216 | tf_op jit(solution)/shard_map/all_to_all | solution.py:96
  41.4 1.6 %sort.46 = (s32[32]{0:T(128)}, s32[32]{0:T(128)S(1)}) sort(s32[32]{0:T(128)S(1)} %reduce, s32[32]{0:T(128)S(1)} %iota.11), dimensions={0}, to_apply=%region_2.3 | sort | flops 160 | bytes 512 | tf_op jit(solution)/shard_map/jit(argsort)/sort | solution.py:102
  43.0 3.9 %all-to-all-done = f32[3,2,32,256]{3,1,0,2:T(2,128)S(1)} async-done(((f32[3,2,32,256]{3,1,0,2:T(2,128)}), f32[3,2,32,256]{3,1,0,2:T(2,128)S(1)}, u32[]{:S(2)}, u32[]{:S(2)}) %all-to-all-start) | async-done | bytes 196640 | tf_op jit(solution)/shard_map/all_to_all | solution.py:96
  49.8 2.6 %collective-permute-start.1 = (f32[6,2,1,512]{3,2,1,0:T(1,128)S(1)}, f32[6,2,1,512]{3,2,1,0:T(1,128)S(1)}, u32[]{:S(2)}, u32[]{:S(2)}) collective-permute-start(f32[6,2,1,512]{3,2,1,0:T(1,128)S(1)} %get-tuple-element.23), channel_id=1, source_target_pairs={{4,0},{8,4},{12,8},{16,12},{20,16},{24,20},{28,24},{0,28},{5,1},{9... | collective-permute-start | bytes 73736 | tf_op jit(solution)/shard_map/ppermute | solution.py:17
  52.4 1.7 %collective-permute-done = f32[6,2,1,512]{3,2,1,0:T(1,128)S(1)} collective-permute-done((f32[6,2,1,512]{3,2,1,0:T(1,128)S(1)}, f32[6,2,1,512]{3,2,1,0:T(1,128)S(1)}, u32[]{:S(2)}, u32[]{:S(2)}) %collective-permute-start) | collective-permute-done | bytes 24608 | tf_op jit(solution)/shard_map/ppermute | solution.py:16
  54.3 1.6 %collective-permute-start.3 = (f32[6,1,18,512]{3,2,1,0:T(8,128)S(1)}, f32[6,1,18,512]{3,2,1,0:T(8,128)S(1)}, u32[]{:S(2)}, u32[]{:S(2)}) collective-permute-start(f32[6,1,18,512]{3,2,1,0:T(8,128)S(1)} %get-tuple-element.20), channel_id=1, source_target_pairs={{0,1},{1,2},{2,3},{3,0},{4,5},{5,6},{6,7},{7,4},{8,9},{9,10},{10,1... | collective-permute-start | bytes 663560 | tf_op jit(solution)/shard_map/ppermute | solution.py:16
  55.9 2.3 %collective-permute-start.2 = (f32[6,1,18,512]{3,2,1,0:T(8,128)S(1)}, f32[6,1,18,512]{3,2,1,0:T(8,128)S(1)}, u32[]{:S(2)}, u32[]{:S(2)}) collective-permute-start(f32[6,1,18,512]{3,2,1,0:T(8,128)S(1)} %get-tuple-element.21), channel_id=1, source_target_pairs={{1,0},{2,1},{3,2},{0,3},{5,4},{6,5},{7,6},{4,7},{9,8},{10,9},{11,1... | collective-permute-start | bytes 663560 | tf_op jit(solution)/shard_map/ppermute | solution.py:17
  59.0 7.1 %collective-permute-done.3 = f32[6,1,18,512]{3,2,1,0:T(8,128)S(1)} collective-permute-done((f32[6,1,18,512]{3,2,1,0:T(8,128)S(1)}, f32[6,1,18,512]{3,2,1,0:T(8,128)S(1)}, u32[]{:S(2)}, u32[]{:S(2)}) %collective-permute-start.3) | collective-permute-done | bytes 221216 | tf_op jit(solution)/shard_map/ppermute | solution.py:16
  66.0 4.7 %collective-permute-done.2 = f32[6,1,18,512]{3,2,1,0:T(8,128)S(1)} collective-permute-done((f32[6,1,18,512]{3,2,1,0:T(8,128)S(1)}, f32[6,1,18,512]{3,2,1,0:T(8,128)S(1)}, u32[]{:S(2)}, u32[]{:S(2)}) %collective-permute-start.2) | collective-permute-done | bytes 221216 | tf_op jit(solution)/shard_map/ppermute | solution.py:17
  75.3 1.4 %maximum_bitcast_fusion = f32[3,2,32,16,16]{4,2,3,1,0:T(8,128)S(1)} fusion(f32[1,2,16,32,16]{4,3,2,1,0:T(8,128)} %stack.23, f32[1,2,16,32,16]{4,3,2,1,0:T(8,128)} %stack.22, f32[1,2,16,32,16]{4,3,2,1,0:T(8,128)S(1)} %stack.10), kind=kLoop, calls=%fused_computation.5 | loop fusion | flops 98304 | bytes 393216 | tf_op jit(solution)/shard_map/transpose | solution.py:72
  77.5 1.5 %gather_fusion.3 = f32[32,3,2,256]{3,2,1,0:T(2,128)} fusion(f32[3,2,32,256]{3,1,2,0:T(2,128)S(1)} %copy.40, s32[1024]{0:T(1024)S(1)} %pad_clamp_fusion.1), kind=kCustom, calls=%fused_computation.3 | custom fusion | bytes 393344 | tf_op jit(solution)/shard_map/gather | solution.py:113
  78.9 3.4 %all-to-all-start.2 = ((f32[3,2,32,256]{3,1,0,2:T(2,128)}), f32[3,2,32,256]{3,1,0,2:T(2,128)S(1)}, u32[]{:S(2)}, u32[]{:S(2)}) async-start(f32[3,2,32,256]{3,1,0,2:T(2,128)} %bitcast.11), calls=%async_computation.2 | async-start | bytes 393216 | tf_op jit(solution)/shard_map/all_to_all | solution.py:116
  83.5 5.0 %all-to-all-done.2 = f32[3,2,32,256]{3,1,0,2:T(2,128)S(1)} async-done(((f32[3,2,32,256]{3,1,0,2:T(2,128)}), f32[3,2,32,256]{3,1,0,2:T(2,128)S(1)}, u32[]{:S(2)}, u32[]{:S(2)}) %all-to-all-start.2) | async-done | bytes 196640 | tf_op jit(solution)/shard_map/all_to_all | solution.py:116
  89.8 3.2 %broadcast_in_dim.19 = f32[3,2,2,32,16,2,16,2]{3,7,6,5,4,2,1,0:T(2,128)S(1)} broadcast(f32[3,2,32,16,16]{2,4,3,1,0:T(8,128)S(1)} %bitcast.35), dimensions={0,1,3,4,6} | broadcast | bytes 1769472 | tf_op jit(solution)/shard_map/broadcast_in_dim | solution.py:118
  93.0 6.3 %add.55 = f32[3,4,32,1024]{2,3,1,0:T(8,128)} add(f32[3,4,32,1024]{2,3,1,0:T(8,128)} %copy.43, f32[3,4,32,1024]{2,3,1,0:T(8,128)S(1)} %bitcast.33) | non-fusion elementwise | flops 393216 | bytes 4718592 | tf_op jit(solution)/shard_map/add | solution.py:122
  99.3 5.5 %copy.44 = f32[3,4,32,1024]{3,2,1,0:T(8,128)} copy(f32[3,4,32,1024]{2,3,1,0:T(8,128)} %add.55) | data formatting | bytes 3145728
  (95 shorter events, 18.4 us)
Async XLA Ops:
  0.6 12.9 %copy-start = (f32[3,4,32,1024]{3,2,1,0:T(8,128)S(1)}, f32[3,4,32,1024]{3,2,1,0:T(8,128)}, u32[]{:S(2)}) copy-start(f32[3,4,32,1024]{3,2,1,0:T(8,128)} %param.3) | copy-start | bytes 4718596
  4.3 8.1 %copy-start.18 = (s32[1024]{0:T(1024)}, s32[1024]{0:T(1024)S(1)}, u32[]{:S(2)}) copy-start(s32[1024]{0:T(1024)S(1)} %pad_clamp_fusion.3) | copy-start | bytes 12292
  5.7 30.8 %all-to-all-start.1 = ((s32[1,1,32,1]{3,1,0,2:T(1,128)}), s32[1,1,32,1]{3,1,0,2:T(1,128)S(1)}, u32[]{:S(2)}, u32[]{:S(2)}) async-start(s32[1,1,32,1]{3,1,0,2:T(1,128)} %copy.33), calls=%async_computation.1 | async-start | bytes 32768 | tf_op jit(solution)/shard_map/all_to_all | solution.py:99
  13.6 21.2 %copy-start.2 = (f32[3,2,16,511]{3,2,1,0:T(8,128)}, f32[3,2,16,511]{3,2,1,0:T(8,128)S(1)}, u32[]{:S(2)}) copy-start(f32[3,2,16,511]{3,2,1,0:T(8,128)S(1)} %get-tuple-element.37) | copy-start | bytes 588676
  36.5 10.4 %all-to-all-start = ((f32[3,2,32,256]{3,1,0,2:T(2,128)}), f32[3,2,32,256]{3,1,0,2:T(2,128)S(1)}, u32[]{:S(2)}, u32[]{:S(2)}) async-start(f32[3,2,32,256]{3,1,0,2:T(2,128)} %copy.32), calls=%async_computation | async-start | bytes 393216 | tf_op jit(solution)/shard_map/all_to_all | solution.py:96
  48.3 1.3 %copy-start.1 = (f32[3,2,16,512]{3,2,1,0:T(8,128)S(1)}, f32[3,2,16,512]{3,2,1,0:T(8,128)}, u32[]{:S(2)}) copy-start(f32[3,2,16,512]{3,2,1,0:T(8,128)} %param.4) | copy-start | bytes 589828
  49.7 4.4 %collective-permute-start = (f32[6,2,1,512]{3,2,1,0:T(1,128)S(1)}, f32[6,2,1,512]{3,2,1,0:T(1,128)S(1)}, u32[]{:S(2)}, u32[]{:S(2)}) collective-permute-start(f32[6,2,1,512]{3,2,1,0:T(1,128)S(1)} %get-tuple-element.22), channel_id=1, source_target_pairs={{0,4},{4,8},{8,12},{12,16},{16,20},{20,24},{24,28},{28,0},{1,5},{5... | collective-permute-start | bytes 73736 | tf_op jit(solution)/shard_map/ppermute | solution.py:16
  49.8 4.4 %collective-permute-start.1 = (f32[6,2,1,512]{3,2,1,0:T(1,128)S(1)}, f32[6,2,1,512]{3,2,1,0:T(1,128)S(1)}, u32[]{:S(2)}, u32[]{:S(2)}) collective-permute-start(f32[6,2,1,512]{3,2,1,0:T(1,128)S(1)} %get-tuple-element.23), channel_id=1, source_target_pairs={{4,0},{8,4},{12,8},{16,12},{20,16},{24,20},{28,24},{0,28},{5,1},{9... | collective-permute-start | bytes 73736 | tf_op jit(solution)/shard_map/ppermute | solution.py:17
  54.1 18.8 %copy-start.4 = (f32[6,2,1,512]{3,2,1,0:T(1,128)}, f32[6,2,1,512]{3,2,1,0:T(1,128)S(1)}, u32[]{:S(2)}) copy-start(f32[6,2,1,512]{3,2,1,0:T(1,128)S(1)} %collective-permute-done) | copy-start | bytes 73732
  54.1 18.8 %copy-start.6 = (f32[6,2,1,512]{3,2,1,0:T(1,128)}, f32[6,2,1,512]{3,2,1,0:T(1,128)S(1)}, u32[]{:S(2)}) copy-start(f32[6,2,1,512]{3,2,1,0:T(1,128)S(1)} %collective-permute-done.1) | copy-start | bytes 73732
  54.3 11.8 %collective-permute-start.3 = (f32[6,1,18,512]{3,2,1,0:T(8,128)S(1)}, f32[6,1,18,512]{3,2,1,0:T(8,128)S(1)}, u32[]{:S(2)}, u32[]{:S(2)}) collective-permute-start(f32[6,1,18,512]{3,2,1,0:T(8,128)S(1)} %get-tuple-element.20), channel_id=1, source_target_pairs={{0,1},{1,2},{2,3},{3,0},{4,5},{5,6},{6,7},{7,4},{8,9},{9,10},{10,1... | collective-permute-start | bytes 663560 | tf_op jit(solution)/shard_map/ppermute | solution.py:16
  55.9 14.8 %collective-permute-start.2 = (f32[6,1,18,512]{3,2,1,0:T(8,128)S(1)}, f32[6,1,18,512]{3,2,1,0:T(8,128)S(1)}, u32[]{:S(2)}, u32[]{:S(2)}) collective-permute-start(f32[6,1,18,512]{3,2,1,0:T(8,128)S(1)} %get-tuple-element.21), channel_id=1, source_target_pairs={{1,0},{2,1},{3,2},{0,3},{5,4},{6,5},{7,6},{4,7},{9,8},{10,9},{11,1... | collective-permute-start | bytes 663560 | tf_op jit(solution)/shard_map/ppermute | solution.py:17
  77.1 5.2 %copy-start.8 = (f32[3,2,16,511]{3,2,1,0:T(8,128)S(1)}, f32[3,2,16,511]{3,2,1,0:T(8,128)}, u32[]{:S(2)}) copy-start(f32[3,2,16,511]{3,2,1,0:T(8,128)} %get-tuple-element.34) | copy-start | bytes 588676
  77.1 5.2 %copy-start.9 = (f32[3,2,16,511]{3,2,1,0:T(8,128)S(1)}, f32[3,2,16,511]{3,2,1,0:T(8,128)}, u32[]{:S(2)}) copy-start(f32[3,2,16,511]{3,2,1,0:T(8,128)} %get-tuple-element.35) | copy-start | bytes 588676
  77.1 5.2 %copy-start.16 = (f32[3,2,16,1]{3,2,1,0:T(8,128)S(1)}, f32[3,2,16,1]{3,2,1,0:T(8,128)}, u32[]{:S(2)}) copy-start(f32[3,2,16,1]{3,2,1,0:T(8,128)} %get-tuple-element.32) | copy-start | bytes 1156
  77.1 5.2 %copy-start.17 = (f32[3,2,16,1]{3,2,1,0:T(8,128)S(1)}, f32[3,2,16,1]{3,2,1,0:T(8,128)}, u32[]{:S(2)}) copy-start(f32[3,2,16,1]{3,2,1,0:T(8,128)} %get-tuple-element.33) | copy-start | bytes 1156
  77.2 5.4 %copy-start.10 = (f32[3,2,16,512]{3,2,1,0:T(8,128)S(1)}, f32[3,2,16,512]{3,2,1,0:T(8,128)}, u32[]{:S(2)}) copy-start(f32[3,2,16,512]{3,2,1,0:T(8,128)} %fusion.3) | copy-start | bytes 589828
  77.2 5.4 %copy-start.11 = (f32[3,2,16,512]{3,2,1,0:T(8,128)S(1)}, f32[3,2,16,512]{3,2,1,0:T(8,128)}, u32[]{:S(2)}) copy-start(f32[3,2,16,512]{3,2,1,0:T(8,128)} %get-tuple-element.30) | copy-start | bytes 589828
  77.2 5.4 %copy-start.3 = (f32[3,2,16,511]{3,2,1,0:T(8,128)S(1)}, f32[3,2,16,511]{3,2,1,0:T(8,128)}, u32[]{:S(2)}) copy-start(f32[3,2,16,511]{3,2,1,0:T(8,128)} %copy-done.2) | copy-start | bytes 588676
  77.2 5.4 %copy-start.5 = (f32[6,2,1,512]{3,2,1,0:T(1,128)S(1)}, f32[6,2,1,512]{3,2,1,0:T(1,128)}, u32[]{:S(2)}) copy-start(f32[6,2,1,512]{3,2,1,0:T(1,128)} %copy-done.4) | copy-start | bytes 73732
  77.2 5.4 %copy-start.7 = (f32[6,2,1,512]{3,2,1,0:T(1,128)S(1)}, f32[6,2,1,512]{3,2,1,0:T(1,128)}, u32[]{:S(2)}) copy-start(f32[6,2,1,512]{3,2,1,0:T(1,128)} %copy-done.6) | copy-start | bytes 73732
  77.2 5.4 %copy-start.13 = (f32[3,2,16,1]{3,2,1,0:T(8,128)S(1)}, f32[3,2,16,1]{3,2,1,0:T(8,128)}, u32[]{:S(2)}) copy-start(f32[3,2,16,1]{3,2,1,0:T(8,128)} %get-tuple-element.38) | copy-start | bytes 1156
  77.2 5.4 %copy-start.15 = (f32[3,2,16,1]{3,2,1,0:T(8,128)S(1)}, f32[3,2,16,1]{3,2,1,0:T(8,128)}, u32[]{:S(2)}) copy-start(f32[3,2,16,1]{3,2,1,0:T(8,128)} %get-tuple-element.39) | copy-start | bytes 1156
  78.9 9.5 %all-to-all-start.2 = ((f32[3,2,32,256]{3,1,0,2:T(2,128)}), f32[3,2,32,256]{3,1,0,2:T(2,128)S(1)}, u32[]{:S(2)}, u32[]{:S(2)}) async-start(f32[3,2,32,256]{3,1,0,2:T(2,128)} %bitcast.11), calls=%async_computation.2 | async-start | bytes 393216 | tf_op jit(solution)/shard_map/all_to_all | solution.py:116
  (3 other events, 2.2 us)
where the time goes:
time: 106 us; the launch traced here: 105 us
  local copies, waits for them, and re-layouts  35.8 us (34%)
  other arithmetic  26.2 us (25%)
  waiting for transfers between devices  22.3 us (21%)
  starting transfers between devices  19.4 us (18%)
  between operations  1.12 us (1%)
    unnamed x42, local copies, waits for them, and re-layouts  10.9 us
    ppermute x2, waiting for transfers between devices, with_halo(): before = lax.ppermute(last, axis, up)  8.8 us
    reduce_sum x1, other arithmetic, restrict(): jnp.sum(v, axis=(2, 5, 7)) * 0.125  7.27 us
    gather x2, local copies, waits for them, and re-layouts, body(): ordered = velocity[:, :, sorted_positions]  6.93 us
    add x1, other arithmetic, body(): velocity + 0.1 * widened_tiles.reshape(3, coarse_depth_index * 2, slot_co...  6.28 us
    all_to_all x1, starting transfers between devices, body(): lax.all_to_all(dispatched_columns, 'xy', split_axis=2, concat_axis=2, til...  5.2 us
    all_to_all x1, waiting for transfers between devices, body(): lax.all_to_all(returned_back_tiles, 'xy', split_axis=2, concat_axis=2, ti...  4.99 us
    ppermute x2, starting transfers between devices, with_halo(): after = lax.ppermute(first, axis, down)  4.9 us
  transfers between devices with their start and end apart: 7, of which 5 were waited for; matrix products, arithmetic and copies ran while one was open for 28% of the time, Pallas kernels for 0%

commit v1 on v0

--- a/solution.py
+++ b/solution.py
@@ -93,8 +93,14 @@
     dispatched_columns = column_indices[sorted_positions].reshape(1, 1, slot_count, 1)
     ordered = velocity[:, :, sorted_positions]
     got, received_columns = (
-        lax.all_to_all(
-            restrict(ordered, BLOCK_EDGE), "xy", split_axis=2, concat_axis=2, tiled=True
+        jnp.concatenate(
+            lax.all_to_all(
+                jnp.stack(jnp.split(restrict(ordered, BLOCK_EDGE), lax.psum(1, "xy"), axis=2)),
+                "xy",
+                0,
+                0,
+            ),
+            axis=2,
         ),
         lax.all_to_all(dispatched_columns, "xy", split_axis=2, concat_axis=2, tiled=True),
     )

time: 106 us -> 112 us (1.057)
  local copies, waits for them, and re-layouts: 35.8 us -> 43.7 us
  waiting for transfers between devices: 22.3 us -> 17 us
  other arithmetic: 26.2 us -> 29.9 us
    another operation x0 -> x2, local copies, waits for them, and re-layouts: none -> 5.41 us  [body(): jnp.stack(jnp.split(restrict(ordered, BLOCK_EDGE), lax.psum(1, 'xy'), axi...]
    ppermute x2, waiting for transfers between devices: 8.8 us -> 4.3 us  [with_halo(): before = lax.ppermute(last, axis, up)]
    unnamed x42 -> x33, local copies, waits for them, and re-layouts: 10.9 us -> 14.4 us
    all_to_all x1, waiting for transfers between devices: 4.99 us -> 2.22 us  [body(): lax.all_to_all(returned_back_tiles, 'xy', split_axis=2, concat_axis=2, ti...]
    ppermute x2, waiting for transfers between devices: 4.65 us -> 6.58 us  [with_halo(): after = lax.ppermute(first, axis, down)]
    mul x2, other arithmetic: 0.26 us -> 1.99 us  [along_x(): return (jnp.roll(middle, -1, 3) - jnp.roll(middle, 1, 3)) * 0.5]
    ppermute x2, starting transfers between devices: 1.69 us -> 0.06 us  [with_halo(): before = lax.ppermute(last, axis, up)]
    ppermute x2, starting transfers between devices: 4.9 us -> 6.29 us  [with_halo(): after = lax.ppermute(first, axis, down)]
  transfers between devices with their start and end apart: 7 -> 7, of which waited for: 5 -> 4; matrix products, arithmetic and copies ran while one was open for 28% -> 35% of each run, Pallas kernels for 0% -> 0%
where the time goes in v1:
time: 112 us; the launch traced here: 111 us
  local copies, waits for them, and re-layouts  43.7 us (39%)
  other arithmetic  29.9 us (27%)
  starting transfers between devices  19.4 us (17%)
  waiting for transfers between devices  17 us (15%)
    unnamed x33, local copies, waits for them, and re-layouts  14.4 us
    reduce_sum x1, other arithmetic, restrict(): jnp.sum(v, axis=(2, 5, 7)) * 0.125  7.27 us
    gather x2, local copies, waits for them, and re-layouts, body(): ordered = velocity[:, :, sorted_positions]  6.92 us
    ppermute x2, waiting for transfers between devices, with_halo(): after = lax.ppermute(first, axis, down)  6.58 us
    ppermute x2, starting transfers between devices, with_halo(): after = lax.ppermute(first, axis, down)  6.29 us
    add x1, other arithmetic, body(): velocity + 0.1 * widened_tiles.reshape(3, coarse_depth_index * 2, slot_co...  6.28 us
    another operation x2, local copies, waits for them, and re-layouts, body(): jnp.stack(jnp.split(restrict(ordered, BLOCK_EDGE), lax.psum(1, 'xy'), axi...  5.41 us
    all_to_all x1, starting transfers between devices, body(): lax.all_to_all(dispatched_columns, 'xy', split_axis=2, concat_axis=2, til...  5.2 us
  transfers between devices with their start and end apart: 7, of which 4 were waited for; matrix products, arithmetic and copies ran while one was open for 35% of the time, Pallas kernels for 0%

profile of v1, /device:TPU:0, one launch (start us, length us, event | category | flops | bytes accessed | tf_op | source)
XLA Modules:
  0.0 111.0 jit_solution(12348180995336600977)
XLA Ops:
  1.4 2.3 %sort.45 = (s32[32]{0:T(128)}, s32[32]{0:T(128)S(1)}) sort(s32[32]{0:T(128)} %param.5, s32[32]{0:T(128)S(1)} %iota.10), dimensions={0}, to_apply=%region_0.1 | sort | flops 160 | bytes 512 | tf_op jit(solution)/shard_map/jit(argsort)/sort | solution.py:92
  5.6 5.2 %all-to-all-start.1 = ((s32[1,1,32,1]{3,1,0,2:T(1,128)}), s32[1,1,32,1]{3,1,0,2:T(1,128)S(1)}, u32[]{:S(2)}, u32[]{:S(2)}) async-start(s32[1,1,32,1]{3,1,0,2:T(1,128)} %copy.64), calls=%async_computation.1 | async-start | bytes 32768 | tf_op jit(solution)/shard_map/all_to_all | solution.py:105
  12.0 1.6 %fusion.22 = (f32[3,2,16,1]{3,2,1,0:T(8,128)}, f32[3,2,16,1]{3,2,1,0:T(8,128)}) fusion(f32[3,2,16,512]{3,2,1,0:T(8,128)} %param.4), kind=kLoop, calls=%fused_computation.98 | loop fusion | bytes 1536 | tf_op jit(solution)/shard_map/jit(_roll_static)/slice | solution.py:45
  13.5 3.0 %gather_fusion = f32[32,3,4,1024]{3,0,2,1:T(8,128)S(1)} fusion(f32[3,4,32,1024]{3,2,1,0:T(8,128)S(1)} %copy-done, s32[1024]{0:T(1024)} %copy-done.9), kind=kCustom, calls=%fused_computation | custom fusion | bytes 3145856 | tf_op jit(solution)/shard_map/gather | solution.py:94
  16.5 4.0 %copy.61 = f32[3,4,32,1024]{2,3,1,0:T(8,128)} copy(f32[3,4,32,1024]{3,2,1,0:T(8,128)S(1)} %bitcast.76) | data formatting | bytes 3145728 | tf_op jit(solution)/shard_map/gather | solution.py:94
  20.5 7.3 %reduce_sum.9 = f32[3,2,32,16,16]{2,4,3,1,0:T(8,128)S(1)} reduce(f32[3,2,2,32,16,2,16,2]{3,7,6,5,4,2,1,0:T(2,128)} %bitcast.74, f32[]{:T(128)} %constant.10.clone.1), dimensions={2,5,7}, to_apply=%region_1.2 | reduce | flops 344064 | bytes 1769476 | tf_op jit(solution)/shard_map/reduce_sum | solution.py:26
  29.8 2.6 %copy-done.2 = f32[8,3,2,4,256]{3,4,2,1,0:T(8,128)} copy-done((f32[8,3,2,4,256]{3,4,2,1,0:T(8,128)}, f32[8,3,2,4,256]{3,4,2,1,0:T(8,128)S(1)}, u32[]{:S(2)}) %copy-start.2) | copy-done | bytes 196632
  32.5 1.6 %sort.47 = (s32[32]{0:T(128)}, s32[32]{0:T(128)S(1)}) sort(s32[32]{0:T(128)S(1)} %copy-done.11, s32[32]{0:T(128)S(1)} %iota.12), dimensions={0}, to_apply=%region_3.4 | sort | flops 160 | bytes 512 | tf_op jit(solution)/shard_map/jit(argsort)/sort | solution.py:123
  35.5 5.1 %copy.62 = f32[8,3,2,4,256]{4,3,2,1,0:T(4,128)} copy(f32[8,3,2,4,256]{3,4,2,1,0:T(8,128)} %copy-done.2) | data formatting | bytes 393216 | tf_op jit(solution)/shard_map/stack | solution.py:98
  40.6 4.2 %all-to-all-start = ((f32[8,3,2,4,256]{4,3,2,1,0:T(4,128)}), f32[8,3,2,4,256]{4,3,2,1,0:T(4,128)S(1)}, u32[]{:S(2)}, u32[]{:S(2)}) async-start(f32[8,3,2,4,256]{4,3,2,1,0:T(4,128)} %copy.62), calls=%async_computation | async-start | bytes 393216 | tf_op jit(solution)/shard_map/all_to_all | solution.py:97
  45.5 1.6 %sort.46 = (s32[32]{0:T(128)}, s32[32]{0:T(128)S(1)}) sort(s32[32]{0:T(128)S(1)} %reduce, s32[32]{0:T(128)S(1)} %iota.11), dimensions={0}, to_apply=%region_2.3 | sort | flops 160 | bytes 512 | tf_op jit(solution)/shard_map/jit(argsort)/sort | solution.py:108
  47.1 3.9 %all-to-all-done = f32[8,3,2,4,256]{4,3,2,1,0:T(4,128)S(1)} async-done(((f32[8,3,2,4,256]{4,3,2,1,0:T(4,128)}), f32[8,3,2,4,256]{4,3,2,1,0:T(4,128)S(1)}, u32[]{:S(2)}, u32[]{:S(2)}) %all-to-all-start) | async-done | bytes 196640 | tf_op jit(solution)/shard_map/all_to_all | solution.py:97
  53.9 2.6 %collective-permute-start.1 = (f32[6,2,1,512]{3,2,1,0:T(1,128)S(1)}, f32[6,2,1,512]{3,2,1,0:T(1,128)S(1)}, u32[]{:S(2)}, u32[]{:S(2)}) collective-permute-start(f32[6,2,1,512]{3,2,1,0:T(1,128)S(1)} %get-tuple-element.25), channel_id=1, source_target_pairs={{4,0},{8,4},{12,8},{16,12},{20,16},{24,20},{28,24},{0,28},{5,1},{9... | collective-permute-start | bytes 73736 | tf_op jit(solution)/shard_map/ppermute | solution.py:17
  57.2 4.0 %copy.73 = f32[3,4,32,1024]{2,3,1,0:T(8,128)} copy(f32[3,4,32,1024]{3,2,1,0:T(8,128)S(1)} %copy-done) | data formatting | bytes 3145728 | tf_op args[0]
  61.4 3.7 %collective-permute-start.2 = (f32[6,1,18,512]{3,2,1,0:T(8,128)S(1)}, f32[6,1,18,512]{3,2,1,0:T(8,128)S(1)}, u32[]{:S(2)}, u32[]{:S(2)}) collective-permute-start(f32[6,1,18,512]{3,2,1,0:T(8,128)S(1)} %get-tuple-element.23), channel_id=1, source_target_pairs={{1,0},{2,1},{3,2},{0,3},{5,4},{6,5},{7,6},{4,7},{9,8},{10,9},{11,1... | collective-permute-start | bytes 663560 | tf_op jit(solution)/shard_map/ppermute | solution.py:17
  65.8 6.6 %collective-permute-done.2 = f32[6,1,18,512]{3,2,1,0:T(8,128)S(1)} collective-permute-done((f32[6,1,18,512]{3,2,1,0:T(8,128)S(1)}, f32[6,1,18,512]{3,2,1,0:T(8,128)S(1)}, u32[]{:S(2)}, u32[]{:S(2)}) %collective-permute-start.2) | collective-permute-done | bytes 221216 | tf_op jit(solution)/shard_map/ppermute | solution.py:17
  72.4 4.3 %collective-permute-done.3 = f32[6,1,18,512]{3,2,1,0:T(8,128)S(1)} collective-permute-done((f32[6,1,18,512]{3,2,1,0:T(8,128)S(1)}, f32[6,1,18,512]{3,2,1,0:T(8,128)S(1)}, u32[]{:S(2)}, u32[]{:S(2)}) %collective-permute-start.3) | collective-permute-done | bytes 221216 | tf_op jit(solution)/shard_map/ppermute | solution.py:16
  83.5 1.5 %gather_fusion.3 = f32[32,3,2,256]{3,2,1,0:T(2,128)} fusion(f32[3,2,32,256]{3,1,2,0:T(2,128)S(1)} %copy.70, s32[1024]{0:T(1024)S(1)} %get-tuple-element.42), kind=kCustom, calls=%fused_computation.3 | custom fusion | bytes 393344 | tf_op jit(solution)/shard_map/gather | solution.py:119
  84.9 3.6 %all-to-all-start.2 = ((f32[3,2,32,256]{3,1,0,2:T(2,128)}), f32[3,2,32,256]{3,1,0,2:T(2,128)S(1)}, u32[]{:S(2)}, u32[]{:S(2)}) async-start(f32[3,2,32,256]{3,1,0,2:T(2,128)} %bitcast.21), calls=%async_computation.2 | async-start | bytes 393216 | tf_op jit(solution)/shard_map/all_to_all | solution.py:122
  90.7 1.8 %fusion.14 = f32[3,2,16,512]{3,2,1,0:T(8,128)} fusion(f32[3,2,16,512]{3,2,1,0:T(8,128)S(1)} %copy-done.1, f32[1,2,16,512]{3,2,1,0:T(8,128)S(1)} %get-tuple-element.30, f32[1,2,16,512]{3,2,1,0:T(8,128)S(1)} %get-tuple-element.31, f32[1,2,16,512]{3,2,1,0:T(8,128)S(1)} %get-tuple-element.29, f32[3,2,16,511]{3,2,1,0:T(8,128)} %copy-done.3, ...), kind=kLoop, calls=%fused_computation.59 | loop fusion | flops 1720320 | bytes 1671168 | tf_op jit(solution)/shard_map/add | solution.py:117
  92.6 2.2 %all-to-all-done.2 = f32[3,2,32,256]{3,1,0,2:T(2,128)S(1)} async-done(((f32[3,2,32,256]{3,1,0,2:T(2,128)}), f32[3,2,32,256]{3,1,0,2:T(2,128)S(1)}, u32[]{:S(2)}, u32[]{:S(2)}) %all-to-all-start.2) | async-done | bytes 196640 | tf_op jit(solution)/shard_map/all_to_all | solution.py:122
  96.0 3.2 %broadcast_in_dim.19 = f32[3,2,2,32,16,2,16,2]{3,7,6,5,4,2,1,0:T(2,128)S(1)} broadcast(f32[3,2,32,16,16]{2,4,3,1,0:T(8,128)S(1)} %bitcast.77), dimensions={0,1,3,4,6} | broadcast | bytes 1769472 | tf_op jit(solution)/shard_map/broadcast_in_dim | solution.py:124
  99.2 6.3 %add.55 = f32[3,4,32,1024]{2,3,1,0:T(8,128)} add(f32[3,4,32,1024]{2,3,1,0:T(8,128)} %copy.73, f32[3,4,32,1024]{2,3,1,0:T(8,128)S(1)} %bitcast.75) | non-fusion elementwise | flops 393216 | bytes 4718592 | tf_op jit(solution)/shard_map/add | solution.py:128
  105.5 5.5 %copy.74 = f32[3,4,32,1024]{3,2,1,0:T(8,128)} copy(f32[3,4,32,1024]{2,3,1,0:T(8,128)} %add.55) | data formatting | bytes 3145728
  (86 shorter events, 22.5 us)
Async XLA Ops:
  0.6 12.9 %copy-start = (f32[3,4,32,1024]{3,2,1,0:T(8,128)S(1)}, f32[3,4,32,1024]{3,2,1,0:T(8,128)}, u32[]{:S(2)}) copy-start(f32[3,4,32,1024]{3,2,1,0:T(8,128)} %param.3) | copy-start | bytes 4718596
  3.7 0.5 copy-start.10
  4.2 1.4 %copy-start.9 = (s32[1024]{0:T(1024)}, s32[1024]{0:T(1024)S(1)}, u32[]{:S(2)}) copy-start(s32[1024]{0:T(1024)S(1)} %pad_clamp_fusion.3) | copy-start | bytes 12292
  5.6 35.0 %all-to-all-start.1 = ((s32[1,1,32,1]{3,1,0,2:T(1,128)}), s32[1,1,32,1]{3,1,0,2:T(1,128)S(1)}, u32[]{:S(2)}, u32[]{:S(2)}) async-start(s32[1,1,32,1]{3,1,0,2:T(1,128)} %copy.64), calls=%async_computation.1 | async-start | bytes 32768 | tf_op jit(solution)/shard_map/all_to_all | solution.py:105
  11.9 22.7 %copy-start.3 = (f32[3,2,16,511]{3,2,1,0:T(8,128)}, f32[3,2,16,511]{3,2,1,0:T(8,128)S(1)}, u32[]{:S(2)}) copy-start(f32[3,2,16,511]{3,2,1,0:T(8,128)S(1)} %get-tuple-element.39) | copy-start | bytes 588676
  27.8 4.7 %copy-start.11 = (s32[32]{0:T(128)S(1)}, s32[32]{0:T(128)}, u32[]{:S(2)}) copy-start(s32[32]{0:T(128)} %copy-done.10) | copy-start | bytes 388
  27.8 6.8 %copy-start.7 = (f32[3,2,16,1]{3,2,1,0:T(8,128)S(1)}, f32[3,2,16,1]{3,2,1,0:T(8,128)}, u32[]{:S(2)}) copy-start(f32[3,2,16,1]{3,2,1,0:T(8,128)} %get-tuple-element.40) | copy-start | bytes 1156
  27.8 6.8 %copy-start.8 = (f32[3,2,16,1]{3,2,1,0:T(8,128)S(1)}, f32[3,2,16,1]{3,2,1,0:T(8,128)}, u32[]{:S(2)}) copy-start(f32[3,2,16,1]{3,2,1,0:T(8,128)} %get-tuple-element.41) | copy-start | bytes 1156
  29.8 2.7 %copy-start.2 = (f32[8,3,2,4,256]{3,4,2,1,0:T(8,128)}, f32[8,3,2,4,256]{3,4,2,1,0:T(8,128)S(1)}, u32[]{:S(2)}) copy-start(f32[8,3,2,4,256]{3,4,2,1,0:T(8,128)S(1)} %fusion) | copy-start | bytes 589828
  35.5 18.3 %copy-start.1 = (f32[3,2,16,512]{3,2,1,0:T(8,128)S(1)}, f32[3,2,16,512]{3,2,1,0:T(8,128)}, u32[]{:S(2)}) copy-start(f32[3,2,16,512]{3,2,1,0:T(8,128)} %param.4) | copy-start | bytes 589828
  40.6 10.4 %all-to-all-start = ((f32[8,3,2,4,256]{4,3,2,1,0:T(4,128)}), f32[8,3,2,4,256]{4,3,2,1,0:T(4,128)S(1)}, u32[]{:S(2)}, u32[]{:S(2)}) async-start(f32[8,3,2,4,256]{4,3,2,1,0:T(4,128)} %copy.62), calls=%async_computation | async-start | bytes 393216 | tf_op jit(solution)/shard_map/all_to_all | solution.py:97
  53.9 7.3 %collective-permute-start = (f32[6,2,1,512]{3,2,1,0:T(1,128)S(1)}, f32[6,2,1,512]{3,2,1,0:T(1,128)S(1)}, u32[]{:S(2)}, u32[]{:S(2)}) collective-permute-start(f32[6,2,1,512]{3,2,1,0:T(1,128)S(1)} %get-tuple-element.24), channel_id=1, source_target_pairs={{0,4},{4,8},{8,12},{12,16},{16,20},{20,24},{24,28},{28,0},{1,5},{5... | collective-permute-start | bytes 73736 | tf_op jit(solution)/shard_map/ppermute | solution.py:16
  53.9 7.3 %collective-permute-start.1 = (f32[6,2,1,512]{3,2,1,0:T(1,128)S(1)}, f32[6,2,1,512]{3,2,1,0:T(1,128)S(1)}, u32[]{:S(2)}, u32[]{:S(2)}) collective-permute-start(f32[6,2,1,512]{3,2,1,0:T(1,128)S(1)} %get-tuple-element.25), channel_id=1, source_target_pairs={{4,0},{8,4},{12,8},{16,12},{20,16},{24,20},{28,24},{0,28},{5,1},{9... | collective-permute-start | bytes 73736 | tf_op jit(solution)/shard_map/ppermute | solution.py:17
  57.2 21.8 %copy-start.6 = (f32[3,2,16,512]{3,2,1,0:T(8,128)S(1)}, f32[3,2,16,512]{3,2,1,0:T(8,128)}, u32[]{:S(2)}) copy-start(f32[3,2,16,512]{3,2,1,0:T(8,128)} %subtract_multiply_fusion.1) | copy-start | bytes 589828
  61.2 17.9 %copy-start.4 = (f32[6,2,1,512]{3,2,1,0:T(1,128)}, f32[6,2,1,512]{3,2,1,0:T(1,128)S(1)}, u32[]{:S(2)}) copy-start(f32[6,2,1,512]{3,2,1,0:T(1,128)S(1)} %collective-permute-done) | copy-start | bytes 73732
  61.2 17.9 %copy-start.5 = (f32[6,2,1,512]{3,2,1,0:T(1,128)}, f32[6,2,1,512]{3,2,1,0:T(1,128)S(1)}, u32[]{:S(2)}) copy-start(f32[6,2,1,512]{3,2,1,0:T(1,128)S(1)} %collective-permute-done.1) | copy-start | bytes 73732
  61.4 11.1 %collective-permute-start.2 = (f32[6,1,18,512]{3,2,1,0:T(8,128)S(1)}, f32[6,1,18,512]{3,2,1,0:T(8,128)S(1)}, u32[]{:S(2)}, u32[]{:S(2)}) collective-permute-start(f32[6,1,18,512]{3,2,1,0:T(8,128)S(1)} %get-tuple-element.23), channel_id=1, source_target_pairs={{1,0},{2,1},{3,2},{0,3},{5,4},{6,5},{7,6},{4,7},{9,8},{10,9},{11,1... | collective-permute-start | bytes 663560 | tf_op jit(solution)/shard_map/ppermute | solution.py:17
  65.0 11.7 %collective-permute-start.3 = (f32[6,1,18,512]{3,2,1,0:T(8,128)S(1)}, f32[6,1,18,512]{3,2,1,0:T(8,128)S(1)}, u32[]{:S(2)}, u32[]{:S(2)}) collective-permute-start(f32[6,1,18,512]{3,2,1,0:T(8,128)S(1)} %get-tuple-element.22), channel_id=1, source_target_pairs={{0,1},{1,2},{2,3},{3,0},{4,5},{5,6},{6,7},{7,4},{8,9},{9,10},{10,1... | collective-permute-start | bytes 663560 | tf_op jit(solution)/shard_map/ppermute | solution.py:16
  84.9 9.8 %all-to-all-start.2 = ((f32[3,2,32,256]{3,1,0,2:T(2,128)}), f32[3,2,32,256]{3,1,0,2:T(2,128)S(1)}, u32[]{:S(2)}, u32[]{:S(2)}) async-start(f32[3,2,32,256]{3,1,0,2:T(2,128)} %bitcast.21), calls=%async_computation.2 | async-start | bytes 393216 | tf_op jit(solution)/shard_map/all_to_all | solution.py:122
